TPU v7x, 512 devices: a whole 4x4x16 slice. The times are simulated.
512 devices in a mesh: expert: 64 (over x, z), dp: 4 (over y), test: 2 (over core).
Axes of the slice: x: 4, y: 4, z: 16, core: 2. Of those that a mesh axis runs over, the one named last changes fastest.
Arguments:
- tokens: bfloat16 [16384, 3584], P(('expert', 'dp'), 'test'), may hold values from -6 to 6
- out_grad: bfloat16 [16384, 3584], P(('expert', 'dp'), 'test'), may hold values from -6 to 6
- route_ids: int32 [16384, 8], P(('expert', 'dp')), may hold values from 0 to 255, as said below
- route_slots: int32 [16384, 8], P(('expert', 'dp')), may hold values from -1 to 1, as said below
- route_weight: bfloat16 [16384, 8], P(('expert', 'dp')), may hold values from 0.19921875 to 1
- w_gate: bfloat16 [64, 3584, 1024], P('expert', None, ('dp', 'test')), may hold values from -0.09375 to 0.09375
- w_up: bfloat16 [64, 3584, 1024], P('expert', None, ('dp', 'test')), may hold values from -0.09375 to 0.09375
- w_down: bfloat16 [64, 1024, 3584], P('expert', ('dp', 'test')), may hold values from -0.1875 to 0.1875
- proj_hidden: bfloat16 [64, 64, 1024], P('expert', None, ('dp', 'test')), may hold values from -0.1875 to 0.1875
- proj_grad: bfloat16 [64, 64, 3584], P('expert'), may hold values from -0.09375 to 0.09375
- test_feats: bfloat16 [64, 256, 4096], P('expert', 'test'), may hold values from -0.09375 to 0.09375
Outputs:
- in_grad: bfloat16 [16384, 3584], P(('expert', 'dp'), 'test')
- scores: float32 [16384, 256], P(('expert', 'dp'), 'test')
Inputs may be any that keep to these rules, and one draw needn't show every extreme that they name: `route_ids`: each row names 8 different experts. `route_slots`: A route's slot is -1 exactly when its expert is 64 or more, or when 2 earlier tokens of the same aligned block of 64 rows already take that expert; otherwise it is the number of earlier tokens of that block routed to that expert.
All inputs are finite; a program needn't handle non-finite values.
Results may differ from a plain program's by a relative error of at most 0.0065.
Values may be sent and summed in bfloat16 or wider, within the bound.
A program may use at most 64 MiB of HBM per device.

v0:
```python
import jax
import jax.numpy as jnp
from jax import lax
from jax.sharding import PartitionSpec as P

CAP = 2


def pick_tables(ids_in, slots_in, weights_in, experts):
    live_mask = (slots_in >= 0) & (ids_in < experts)
    slot_code = jnp.where(live_mask, ids_in * CAP + slots_in, -1)
    columns = jnp.arange(experts * CAP, dtype=jnp.int32)
    matches = slot_code[:, :, None] == columns[None, None, :]
    picks = jnp.sum(matches.astype(jnp.float32), axis=1)
    weighted = jnp.sum(jnp.where(matches, weights_in.astype(jnp.float32)[:, :, None], 0.0), axis=1)
    return (picks.astype(jnp.bfloat16), weighted.astype(jnp.bfloat16))


def dot(a, b, ca, cb):
    return lax.dot_general(a, b, (((ca,), (cb,)), ((), ())), preferred_element_type=jnp.float32)


def on_device(
    tokens,
    out_grad,
    route_ids,
    route_slots,
    route_weight,
    w_gate,
    w_up,
    w_down,
    proj_hidden,
    proj_grad,
    test_feats,
):
    experts = lax.axis_size("expert")
    groups = lax.axis_size("dp")
    halves = lax.axis_size("test")
    half = tokens.shape[1]
    slots = experts * CAP
    pick, weighted = pick_tables(route_ids, route_slots, route_weight, experts)
    in_buf = dot(pick, tokens, 0, 0).astype(jnp.bfloat16)
    grad_buf = dot(weighted, out_grad, 0, 0).astype(jnp.bfloat16)

    def exchange(rows):
        width = rows.shape[1]
        moved = lax.all_to_all(
            rows.reshape(experts, CAP, width), "expert", split_axis=0, concat_axis=0, tiled=True
        )
        return moved.reshape(slots, width)

    def spread(rows):
        full = lax.all_gather(rows, ("dp", "test"), axis=0, tiled=True)
        full = full.reshape(groups, halves, slots, half)
        return [full[:, h].reshape(groups * slots, half) for h in range(halves)]

    mine_in = exchange(in_buf)
    ins = spread(mine_in)
    mine_grad = exchange(grad_buf)
    grads = spread(mine_grad)
    gate_w, up_w, down_w = (w_gate[0], w_up[0], w_down[0])

    def cut(arr, h, axis):
        return lax.slice_in_dim(arr, h * half, (h + 1) * half, axis=axis)

    gate_pre = sum((dot(ins[h], cut(gate_w, h, 0), 1, 0) for h in range(halves)))
    up_pre = sum((dot(ins[h], cut(up_w, h, 0), 1, 0) for h in range(halves)))
    sig = jax.nn.sigmoid(gate_pre)
    act = gate_pre * sig
    hidden = (act * up_pre).astype(jnp.bfloat16)
    proj_part = dot(hidden, proj_hidden[0], 1, 1)
    hid_grad = sum((dot(grads[h], cut(down_w, h, 1), 1, 1) for h in range(halves)))
    up_grad = (hid_grad * act).astype(jnp.bfloat16)
    gate_grad = (hid_grad * up_pre * sig * (1.0 + gate_pre * (1.0 - sig))).astype(jnp.bfloat16)
    parts = [
        (dot(gate_grad, cut(gate_w, h, 0), 1, 1) + dot(up_grad, cut(up_w, h, 0), 1, 1)).astype(
            jnp.bfloat16
        )
        for h in range(halves)
    ]
    parts = jnp.stack([p.reshape(groups, slots, half) for p in parts], axis=1)
    mine_back = lax.psum_scatter(
        parts.reshape(groups * halves * slots, half),
        ("dp", "test"),
        scatter_dimension=0,
        tiled=True,
    )
    back = exchange(mine_back.astype(jnp.bfloat16))
    in_grad = dot(pick, back, 1, 0).astype(jnp.bfloat16)
    hidden_vec = lax.psum(proj_part, ("dp", "test"))
    me = lax.axis_index("dp")
    hid_mine = lax.dynamic_slice_in_dim(hidden_vec, me * slots, slots, 0)
    grad_mine = sum(
        (
            dot(
                lax.dynamic_slice_in_dim(grads[h], me * slots, slots, 0),
                cut(proj_grad[0], h, 1),
                1,
                1,
            )
            for h in range(halves)
        )
    )
    feature = (hid_mine[:, :, None] * grad_mine[:, None, :]).reshape(slots, -1).astype(jnp.bfloat16)
    score = dot(feature, test_feats[0], 1, 1).astype(jnp.bfloat16)
    scores = dot(pick, exchange(score), 1, 0)
    return (in_grad, scores)


def solution(mesh):
    placed = (
        P(("expert", "dp"), "test"),
        P(("expert", "dp"), "test"),
        P(("expert", "dp"), None),
        P(("expert", "dp"), None),
        P(("expert", "dp"), None),
        P("expert", None, ("dp", "test")),
        P("expert", None, ("dp", "test")),
        P("expert", ("dp", "test"), None),
        P("expert", None, ("dp", "test")),
        P("expert", None, None),
        P("expert", "test", None),
    )
    return jax.shard_map(
        on_device,
        mesh=mesh,
        in_specs=placed,
        out_specs=(P(("expert", "dp"), "test"), P(("expert", "dp"), "test")),
        check_vma=False,
    )
```

profile of v0, /device:TPU:31, one launch (start us, length us, event | category | flops | bytes accessed | tf_op | source)
XLA Modules:
  0.0 316.4 jit_solution(14806735404021677156)
XLA Ops:
  7.2 0.8 add_select_fusion
  8.0 0.1 copy.21
  8.1 0.8 copy.22
  8.9 0.2 select_reduce_fusion
  9.1 1.3 convolution_convert_fusion.1
  10.4 0.2 reshape.58
  10.6 45.3 %all_to_all.20 = bf16[64,2,1792]{2,1,0:T(2,128)(2,1)S(1)} all-to-all(bf16[64,2,1792]{2,1,0:T(2,128)(2,1)S(1)} %reshape.58), channel_id=1, replica_groups=mesh['expert'=64,'dp'=4,'test'=2] {'expert'}, dimensions={0} | all-to-all | bytes 917504 | tf_op jit(solution)/shard_map/all_to_all | solution.py:47
  55.9 1.0 reshape.59
  56.9 0.3 convolution_convert_fusion
  57.2 0.2 reshape.61
  57.4 34.0 %all_to_all.21 = bf16[64,2,1792]{2,1,0:T(2,128)(2,1)S(1)} all-to-all(bf16[64,2,1792]{2,1,0:T(2,128)(2,1)S(1)} %reshape.61), channel_id=1, replica_groups=mesh['expert'=64,'dp'=4,'test'=2] {'expert'}, dimensions={0} | all-to-all | bytes 917504 | tf_op jit(solution)/shard_map/all_to_all | solution.py:47
  91.4 0.9 reshape.62
  92.4 0.0 all-reduce.2.cloned.1.call-start
  92.4 3.6 %fusion.41 = (bf16[4,1,128,1792]{3,2,1,0:T(8,128)(2,1)}, bf16[4,1,128,1792]{3,2,1,0:T(8,128)(2,1)S(1)}) fusion(bf16[4,2,128,1792]{3,2,1,0:T(8,128)(2,1)} %bitcast.73), kind=kLoop, calls=%fused_computation.61 | loop fusion | bytes 7340032 | tf_op jit(solution)/shard_map/slice | solution.py:55
  96.0 31.3 %all-gather.5.cloned.1.call-done = bf16[1024,1792]{1,0:T(8,128)(2,1)} async-done(((bf16[128,1792]{1,0:T(8,128)(2,1)}), bf16[1024,1792]{1,0:T(8,128)(2,1)}) %all-gather.5.cloned.1.call-update) | async-done | bytes 3670032 | tf_op jit(solution)/shard_map/all_gather | solution.py:53
  127.4 2.4 fusion.42
  129.8 0.6 fusion.9
  130.4 0.5 copy-done.3
  130.9 0.6 fusion.14
  131.6 0.6 convolution_add_fusion.1
  132.3 0.6 convolution_add_fusion
  132.9 0.5 copy-done.7
  133.4 0.6 fusion.2
  134.1 0.4 copy-done.5
  134.5 0.6 multiply_convert_fusion.2
  135.1 2.4 fusion.4
  137.6 2.5 fusion.7
  140.1 0.9 fusion.30
  141.0 3.0 add_convert_fusion
  144.0 0.3 copy-done.1
  144.3 0.2 copy-done.4
  144.5 0.6 add_convert_fusion.1
  145.2 2.1 pad_maximum_fusion
  147.3 1.0 copy-done.6
  148.3 0.3 fusion.17
  148.6 1.3 convolution_add_fusion.3
  149.9 66.4 %all-reduce.2.cloned.1.call-done = f32[512,64]{0,1:T(8,128)} async-done(((f32[512,64]{0,1:T(8,128)}), f32[512,64]{0,1:T(8,128)}) %all-reduce.2.cloned.1.call-update) | async-done | bytes 131088 | tf_op jit(solution)/shard_map/psum | solution.py:90
  216.3 0.8 constant_dynamic-slice_fusion
  217.1 0.3 multiply_convert_fusion
  217.4 1.1 convolution_convert_fusion.3
  218.5 15.3 %all-to-all-start.3 = ((bf16[64,2,128]{2,1,0:T(2,128)(2,1)}), bf16[64,2,128]{2,1,0:T(2,128)(2,1)S(1)}, u32[]{:S(2)}, u32[]{:S(2)}) async-start(bf16[64,2,128]{2,1,0:T(2,128)(2,1)} %bitcast.20), calls=%async_computation.4 | async-start | bytes 65536 | tf_op jit(solution)/shard_map/all_to_all | solution.py:47
  233.8 29.1 %reduce-scatter.2.cloned.1.call-done = bf16[128,1792]{1,0:T(8,128)(2,1)} async-done(((bf16[1024,1792]{1,0:T(8,128)(2,1)}), bf16[128,1792]{1,0:T(8,128)(2,1)}) %reduce-scatter.2.cloned.1.call-update) | async-done | bytes 458768 | tf_op jit(solution)/shard_map/reduce_scatter | solution.py:82
  262.9 2.0 reshape.65
  264.9 15.0 %all-to-all-start.2 = ((bf16[64,2,1792]{2,1,0:T(2,128)(2,1)}), bf16[64,2,1792]{2,1,0:T(2,128)(2,1)S(1)}, u32[]{:S(2)}, u32[]{:S(2)}) async-start(bf16[64,2,1792]{2,1,0:T(2,128)(2,1)} %reshape.65), calls=%async_computation.3 | async-start | bytes 917504 | tf_op jit(solution)/shard_map/all_to_all | solution.py:47
  279.9 0.7 fusion.43
  280.6 28.2 %all-to-all-done.2 = bf16[64,2,1792]{2,1,0:T(2,128)(2,1)S(1)} async-done(((bf16[64,2,1792]{2,1,0:T(2,128)(2,1)}), bf16[64,2,1792]{2,1,0:T(2,128)(2,1)S(1)}, u32[]{:S(2)}, u32[]{:S(2)}) %all-to-all-start.2) | async-done | bytes 458784 | tf_op jit(solution)/shard_map/all_to_all | solution.py:47
  308.8 0.2 reshape.66
  309.0 0.9 convolution_convert_fusion.2
  (23 shorter events, 0.2 us)
Async XLA Ops:
  7.2 210.2 %copy-start = (bf16[1,128,4096]{2,1,0:T(8,128)(2,1)S(1)}, bf16[1,128,4096]{2,1,0:T(8,128)(2,1)}, u32[]{:S(2)}) copy-start(bf16[1,128,4096]{2,1,0:T(8,128)(2,1)} %param.21) | copy-start | bytes 3145732
  7.2 85.2 %all-gather.3.cloned.1.call-start = ((), (), s32[]{:S(2)}) async-start(), calls=%async_computation.5 | async-start | bytes 4128768 | tf_op jit(solution)/shard_map/all_gather | solution.py:53
  9.1 47.8 %copy-start.8 = (bf16[64,1792]{1,0:T(8,128)(2,1)S(1)}, bf16[64,1792]{1,0:T(8,128)(2,1)}, u32[]{:S(2)}) copy-start(bf16[64,1792]{1,0:T(8,128)(2,1)} %param.11) | copy-start | bytes 688132
  56.9 70.5 %all-gather.5.cloned.1.call-start = ((), (), s32[]{:S(2)}) async-start(), calls=%async_computation.6 | async-start | bytes 4128768 | tf_op jit(solution)/shard_map/all_gather | solution.py:53
  92.4 124.0 %all-reduce.2.cloned.1.call-start = ((), (), s32[]{:S(2)}) async-start(), calls=%async_computation.8 | async-start | bytes 262144 | tf_op jit(solution)/shard_map/psum | solution.py:90
  127.4 2.4 copy-start.2
  129.8 1.2 copy-start.3
  132.2 1.2 copy-start.7
  132.9 1.6 copy-start.5
  137.6 2.5 copy-start.9
  140.9 122.0 %reduce-scatter.2.cloned.1.call-start = ((), (), s32[]{:S(2)}) async-start(), calls=%async_computation.7 | async-start | bytes 4128768 | tf_op jit(solution)/shard_map/reduce_scatter | solution.py:82
  141.0 3.3 %copy-start.1 = (f32[512,1792]{1,0:T(8,128)S(1)}, f32[512,1792]{1,0:T(8,128)}, u32[]{:S(2)}) copy-start(f32[512,1792]{1,0:T(8,128)} %fusion.7) | copy-start | bytes 11010052
  141.0 3.5 %copy-start.4 = (bf16[1,3584,128]{2,1,0:T(8,128)(2,1)S(1)}, bf16[1,3584,128]{2,1,0:T(8,128)(2,1)}, u32[]{:S(2)}) copy-start(bf16[1,3584,128]{2,1,0:T(8,128)(2,1)} %param.17) | copy-start | bytes 2752516
  147.3 1.0 copy-start.6
  218.5 46.4 %all-to-all-start.3 = ((bf16[64,2,128]{2,1,0:T(2,128)(2,1)}), bf16[64,2,128]{2,1,0:T(2,128)(2,1)S(1)}, u32[]{:S(2)}, u32[]{:S(2)}) async-start(bf16[64,2,128]{2,1,0:T(2,128)(2,1)} %bitcast.20), calls=%async_computation.4 | async-start | bytes 65536 | tf_op jit(solution)/shard_map/all_to_all | solution.py:47
  264.9 43.9 %all-to-all-start.2 = ((bf16[64,2,1792]{2,1,0:T(2,128)(2,1)}), bf16[64,2,1792]{2,1,0:T(2,128)(2,1)S(1)}, u32[]{:S(2)}, u32[]{:S(2)}) async-start(bf16[64,2,1792]{2,1,0:T(2,128)(2,1)} %reshape.65), calls=%async_computation.3 | async-start | bytes 917504 | tf_op jit(solution)/shard_map/all_to_all | solution.py:47
Sparse Core Ops, SparseCore 0:
  57.0 30.6 all-gather.2
  92.5 34.8 all-gather.4
  141.1 75.2 all-reduce.1
  219.0 43.8 reduce-scatter.1
where the time goes:
time: 317 us; the launch traced here: 316 us
  waiting for transfers between devices  155 us (49%)
  blocking collectives  79.3 us (25%)
  starting transfers between devices  30.5 us (10%)
  matrix products  19.2 us (6%)
  local copies, waits for them, and re-layouts  15 us (5%)
  between operations  14 us (4%)
  other arithmetic  3.41 us (1%)
    all_to_all x2, blocking collectives, exchange(): lax.all_to_all(rows.reshape(experts, CAP, width), 'expert', split_axis=0,...  79.3 us
    psum x1, waiting for transfers between devices, on_device(): hidden_vec = lax.psum(proj_part, ('dp', 'test'))  66.4 us
    all_gather x2, waiting for transfers between devices, spread(): full = lax.all_gather(rows, ('dp', 'test'), axis=0, tiled=True)  31.3 us
    all_to_all x2, starting transfers between devices, exchange(): lax.all_to_all(rows.reshape(experts, CAP, width), 'expert', split_axis=0,...  30.3 us
    reduce_scatter x1, waiting for transfers between devices, on_device(): lax.psum_scatter(parts.reshape(groups * halves * slots, half), ('dp', 'te...  29.1 us
    all_to_all x2, waiting for transfers between devices, exchange(): lax.all_to_all(rows.reshape(experts, CAP, width), 'expert', split_axis=0,...  28.2 us
    dot_general x18, matrix products, dot(): lax.dot_general(a, b, (((ca,), (cb,)), ((), ())), preferred_element_type=...  19.2 us
  transfers between devices with their start and end apart: 6, of which 4 were waited for; matrix products, arithmetic and copies ran while one was open for 5% of the time, Pallas kernels for 0%

commit v1 on v0

--- a/solution.py
+++ b/solution.py
@@ -50,7 +50,19 @@
         return moved.reshape(slots, width)
 
     def spread(rows):
-        full = lax.all_gather(rows, ("dp", "test"), axis=0, tiled=True)
+
+        def hold_the_digits(arr_in, link_axis):
+            return jnp.concatenate(
+                jax.lax.all_to_all(
+                    jnp.stack([arr_in for _ in range(jax.lax.axis_size(link_axis))], axis=0),
+                    link_axis,
+                    0,
+                    0,
+                ),
+                axis=0,
+            )
+
+        full = hold_the_digits(rows, ("dp", "test"))
         full = full.reshape(groups, halves, slots, half)
         return [full[:, h].reshape(groups * slots, half) for h in range(halves)]
 

time: 317 us -> 372 us (1.17)
  waiting for transfers between devices: 155 us -> 244 us
  blocking collectives: 79.3 us -> 0 us
  starting transfers between devices: 30.5 us -> 71.5 us
    all_to_all x2 -> x0, blocking collectives: 79.3 us -> none  [exchange(): lax.all_to_all(rows.reshape(experts, CAP, width), 'expert', split_axis=0,...]
    all_to_all x0 -> x2, waiting for transfers between devices: none -> 76.6 us  [hold_the_digits(): jax.lax.all_to_all(jnp.stack([arr_in for _ in range(jax.lax.axis_size(lin...]
    all_to_all x2 -> x4, waiting for transfers between devices: 28.2 us -> 80.2 us  [exchange(): lax.all_to_all(rows.reshape(experts, CAP, width), 'expert', split_axis=0,...]
    all_gather x2 -> x0, waiting for transfers between devices: 31.3 us -> none  [spread(): full = lax.all_gather(rows, ('dp', 'test'), axis=0, tiled=True)]
    all_to_all x2 -> x4, starting transfers between devices: 30.3 us -> 56.5 us  [exchange(): lax.all_to_all(rows.reshape(experts, CAP, width), 'expert', split_axis=0,...]
    all_to_all x0 -> x2, starting transfers between devices: none -> 15 us  [hold_the_digits(): jax.lax.all_to_all(jnp.stack([arr_in for _ in range(jax.lax.axis_size(lin...]
    psum x1, waiting for transfers between devices: 66.4 us -> 57.5 us  [on_device(): hidden_vec = lax.psum(proj_part, ('dp', 'test'))]
    another operation x0 -> x4, local copies, waits for them, and re-layouts: none -> 4.56 us  [hold_the_digits(): jnp.stack([arr_in for _ in range(jax.lax.axis_size(link_axis))], axis=0)]
  transfers between devices with their start and end apart: 6 -> 8, of which waited for: 4 -> 7; matrix products, arithmetic and copies ran while one was open for 5% -> 5% of each run, Pallas kernels for 0% -> 0%
where the time goes in v1:
time: 372 us; the launch traced here: 371 us
  waiting for transfers between devices  244 us (66%)
  starting transfers between devices  71.5 us (19%)
  matrix products  19.8 us (5%)
  local copies, waits for them, and re-layouts  18.1 us (5%)
  between operations  14.3 us (4%)
    all_to_all x4, waiting for transfers between devices, exchange(): lax.all_to_all(rows.reshape(experts, CAP, width), 'expert', split_axis=0,...  80.2 us
    all_to_all x2, waiting for transfers between devices, hold_the_digits(): jax.lax.all_to_all(jnp.stack([arr_in for _ in range(jax.lax.axis_size(lin...  76.6 us
    psum x1, waiting for transfers between devices, on_device(): hidden_vec = lax.psum(proj_part, ('dp', 'test'))  57.5 us
    all_to_all x4, starting transfers between devices, exchange(): lax.all_to_all(rows.reshape(experts, CAP, width), 'expert', split_axis=0,...  56.5 us
    reduce_scatter x1, waiting for transfers between devices, on_device(): lax.psum_scatter(parts.reshape(groups * halves * slots, half), ('dp', 'te...  29.3 us
    dot_general x18, matrix products, dot(): lax.dot_general(a, b, (((ca,), (cb,)), ((), ())), preferred_element_type=...  19.8 us
    all_to_all x2, starting transfers between devices, hold_the_digits(): jax.lax.all_to_all(jnp.stack([arr_in for _ in range(jax.lax.axis_size(lin...  15 us
  transfers between devices with their start and end apart: 8, of which 7 were waited for; matrix products, arithmetic and copies ran while one was open for 5% of the time, Pallas kernels for 0%

profile of v1, /device:TPU:31, one launch (start us, length us, event | category | flops | bytes accessed | tf_op | source)
XLA Modules:
  0.0 370.7 jit_solution(9035887714529227340)
XLA Ops:
  7.2 0.8 add_select_fusion
  8.1 0.8 copy.22
  9.1 1.2 convolution_convert_fusion
  10.4 1.0 reshape.51
  11.3 18.2 %all-to-all-start.2 = ((bf16[64,2,1792]{2,1,0:T(2,128)(2,1)}), bf16[64,2,1792]{2,1,0:T(2,128)(2,1)S(1)}, u32[]{:S(2)}, u32[]{:S(2)}) async-start(bf16[64,2,1792]{2,1,0:T(2,128)(2,1)} %reshape.51), calls=%async_computation.2 | async-start | bytes 917504 | tf_op jit(solution)/shard_map/all_to_all | solution.py:47
  29.6 0.3 convolution_convert_fusion.1
  29.9 1.0 reshape.50
  30.8 26.0 %all-to-all-done.2 = bf16[64,2,1792]{2,1,0:T(2,128)(2,1)S(1)} async-done(((bf16[64,2,1792]{2,1,0:T(2,128)(2,1)}), bf16[64,2,1792]{2,1,0:T(2,128)(2,1)S(1)}, u32[]{:S(2)}, u32[]{:S(2)}) %all-to-all-start.2) | async-done | bytes 458784 | tf_op jit(solution)/shard_map/all_to_all | solution.py:47
  56.8 7.9 %all-to-all-start = ((bf16[64,2,1792]{2,1,0:T(2,128)(2,1)}), bf16[64,2,1792]{2,1,0:T(2,128)(2,1)S(1)}, u32[]{:S(2)}, u32[]{:S(2)}) async-start(bf16[64,2,1792]{2,1,0:T(2,128)(2,1)} %reshape.50), calls=%async_computation | async-start | bytes 917504 | tf_op jit(solution)/shard_map/all_to_all | solution.py:47
  64.9 26.0 %all-to-all-done = bf16[64,2,1792]{2,1,0:T(2,128)(2,1)S(1)} async-done(((bf16[64,2,1792]{2,1,0:T(2,128)(2,1)}), bf16[64,2,1792]{2,1,0:T(2,128)(2,1)S(1)}, u32[]{:S(2)}, u32[]{:S(2)}) %all-to-all-start) | async-done | bytes 458784 | tf_op jit(solution)/shard_map/all_to_all | solution.py:47
  90.9 2.0 stack.10
  93.0 7.9 %all-to-all-start.3 = ((bf16[8,128,1792]{2,1,0:T(8,128)(2,1)}), bf16[8,128,1792]{2,1,0:T(8,128)(2,1)}, u32[]{:S(2)}, u32[]{:S(2)}) async-start(bf16[8,128,1792]{2,1,0:T(8,128)(2,1)} %stack.10), calls=%async_computation.3 | async-start | bytes 7340032 | tf_op jit(solution)/shard_map/all_to_all | solution.py:56
  101.1 41.3 %all-to-all-done.3 = bf16[8,128,1792]{2,1,0:T(8,128)(2,1)} async-done(((bf16[8,128,1792]{2,1,0:T(8,128)(2,1)}), bf16[8,128,1792]{2,1,0:T(8,128)(2,1)}, u32[]{:S(2)}, u32[]{:S(2)}) %all-to-all-start.3) | async-done | bytes 3670048 | tf_op jit(solution)/shard_map/all_to_all | solution.py:56
  142.4 2.2 stack.9
  144.6 7.1 %all-to-all-start.1 = ((bf16[8,128,1792]{2,1,0:T(8,128)(2,1)}), bf16[8,128,1792]{2,1,0:T(8,128)(2,1)}, u32[]{:S(2)}, u32[]{:S(2)}) async-start(bf16[8,128,1792]{2,1,0:T(8,128)(2,1)} %stack.9), calls=%async_computation.1 | async-start | bytes 7340032 | tf_op jit(solution)/shard_map/all_to_all | solution.py:56
  151.7 2.4 fusion.42
  154.1 0.6 fusion.9
  154.7 0.5 copy-done.4
  155.2 0.6 fusion.14
  155.9 0.6 convolution_add_fusion.1
  156.5 1.3 convolution_add_fusion
  157.9 35.3 %all-to-all-done.1 = bf16[8,128,1792]{2,1,0:T(8,128)(2,1)} async-done(((bf16[8,128,1792]{2,1,0:T(8,128)(2,1)}), bf16[8,128,1792]{2,1,0:T(8,128)(2,1)}, u32[]{:S(2)}, u32[]{:S(2)}) %all-to-all-start.1) | async-done | bytes 3670048 | tf_op jit(solution)/shard_map/all_to_all | solution.py:56
  193.1 2.4 fusion.41
  195.5 0.6 fusion.2
  196.2 0.5 copy-done.8
  196.7 0.6 multiply_convert_fusion.2
  197.3 0.5 copy-done.3
  197.8 2.4 fusion.4
  200.3 2.5 fusion.7
  202.8 0.9 fusion.30
  203.7 3.0 add_convert_fusion
  206.7 0.3 copy-done.1
  207.2 0.7 add_convert_fusion.1
  207.9 2.1 pad_maximum_fusion
  210.0 1.0 copy-done.7
  211.0 0.3 fusion.17
  211.3 1.3 convolution_add_fusion.3
  212.6 57.5 %all-reduce.2.cloned.1.call-done = f32[512,64]{0,1:T(8,128)} async-done(((f32[512,64]{0,1:T(8,128)}), f32[512,64]{0,1:T(8,128)}) %all-reduce.2.cloned.1.call-update) | async-done | bytes 131088 | tf_op jit(solution)/shard_map/psum | solution.py:102
  270.1 0.8 constant_dynamic-slice_fusion
  270.9 0.3 multiply_convert_fusion
  271.2 1.1 convolution_convert_fusion.3
  272.3 15.3 %all-to-all-start.5 = ((bf16[64,2,128]{2,1,0:T(2,128)(2,1)}), bf16[64,2,128]{2,1,0:T(2,128)(2,1)S(1)}, u32[]{:S(2)}, u32[]{:S(2)}) async-start(bf16[64,2,128]{2,1,0:T(2,128)(2,1)} %bitcast.20), calls=%async_computation.6 | async-start | bytes 65536 | tf_op jit(solution)/shard_map/all_to_all | solution.py:47
  287.7 29.3 %reduce-scatter.2.cloned.1.call-done = bf16[128,1792]{1,0:T(8,128)(2,1)} async-done(((bf16[1024,1792]{1,0:T(8,128)(2,1)}), bf16[128,1792]{1,0:T(8,128)(2,1)}) %reduce-scatter.2.cloned.1.call-update) | async-done | bytes 458768 | tf_op jit(solution)/shard_map/reduce_scatter | solution.py:94
  316.9 2.0 reshape.53
  318.9 15.0 %all-to-all-start.4 = ((bf16[64,2,1792]{2,1,0:T(2,128)(2,1)}), bf16[64,2,1792]{2,1,0:T(2,128)(2,1)S(1)}, u32[]{:S(2)}, u32[]{:S(2)}) async-start(bf16[64,2,1792]{2,1,0:T(2,128)(2,1)} %reshape.53), calls=%async_computation.5 | async-start | bytes 917504 | tf_op jit(solution)/shard_map/all_to_all | solution.py:47
  333.8 0.7 fusion.43
  334.6 28.2 %all-to-all-done.4 = bf16[64,2,1792]{2,1,0:T(2,128)(2,1)S(1)} async-done(((bf16[64,2,1792]{2,1,0:T(2,128)(2,1)}), bf16[64,2,1792]{2,1,0:T(2,128)(2,1)S(1)}, u32[]{:S(2)}, u32[]{:S(2)}) %all-to-all-start.4) | async-done | bytes 458784 | tf_op jit(solution)/shard_map/all_to_all | solution.py:47
  362.9 0.9 convolution_convert_fusion.2
  (29 shorter events, 1.2 us)
Async XLA Ops:
  7.2 264.0 %copy-start = (bf16[1,128,4096]{2,1,0:T(8,128)(2,1)S(1)}, bf16[1,128,4096]{2,1,0:T(8,128)(2,1)}, u32[]{:S(2)}) copy-start(bf16[1,128,4096]{2,1,0:T(8,128)(2,1)} %param.21) | copy-start | bytes 3145732
  7.2 22.4 %copy-start.10 = (bf16[64,1792]{1,0:T(8,128)(2,1)S(1)}, bf16[64,1792]{1,0:T(8,128)(2,1)}, u32[]{:S(2)}) copy-start(bf16[64,1792]{1,0:T(8,128)(2,1)} %param.12) | copy-start | bytes 688132
  11.3 45.5 %all-to-all-start.2 = ((bf16[64,2,1792]{2,1,0:T(2,128)(2,1)}), bf16[64,2,1792]{2,1,0:T(2,128)(2,1)S(1)}, u32[]{:S(2)}, u32[]{:S(2)}) async-start(bf16[64,2,1792]{2,1,0:T(2,128)(2,1)} %reshape.51), calls=%async_computation.2 | async-start | bytes 917504 | tf_op jit(solution)/shard_map/all_to_all | solution.py:47
  56.8 34.1 %all-to-all-start = ((bf16[64,2,1792]{2,1,0:T(2,128)(2,1)}), bf16[64,2,1792]{2,1,0:T(2,128)(2,1)S(1)}, u32[]{:S(2)}, u32[]{:S(2)}) async-start(bf16[64,2,1792]{2,1,0:T(2,128)(2,1)} %reshape.50), calls=%async_computation | async-start | bytes 917504 | tf_op jit(solution)/shard_map/all_to_all | solution.py:47
  93.0 49.4 %all-to-all-start.3 = ((bf16[8,128,1792]{2,1,0:T(8,128)(2,1)}), bf16[8,128,1792]{2,1,0:T(8,128)(2,1)}, u32[]{:S(2)}, u32[]{:S(2)}) async-start(bf16[8,128,1792]{2,1,0:T(8,128)(2,1)} %stack.10), calls=%async_computation.3 | async-start | bytes 7340032 | tf_op jit(solution)/shard_map/all_to_all | solution.py:56
  144.6 48.5 %all-to-all-start.1 = ((bf16[8,128,1792]{2,1,0:T(8,128)(2,1)}), bf16[8,128,1792]{2,1,0:T(8,128)(2,1)}, u32[]{:S(2)}, u32[]{:S(2)}) async-start(bf16[8,128,1792]{2,1,0:T(8,128)(2,1)} %stack.9), calls=%async_computation.1 | async-start | bytes 7340032 | tf_op jit(solution)/shard_map/all_to_all | solution.py:56
  151.6 118.5 %all-reduce.2.cloned.1.call-start = ((), (), s32[]{:S(2)}) async-start(), calls=%async_computation.8 | async-start | bytes 262144 | tf_op jit(solution)/shard_map/psum | solution.py:102
  151.7 2.4 copy-start.2
  154.0 1.2 copy-start.4
  193.1 2.4 copy-start.9
  195.5 1.8 copy-start.6
  195.5 1.1 copy-start.8
  196.7 1.2 copy-start.3
  200.3 2.5 copy-start.11
  203.7 113.2 %reduce-scatter.2.cloned.1.call-start = ((), (), s32[]{:S(2)}) async-start(), calls=%async_computation.7 | async-start | bytes 4128768 | tf_op jit(solution)/shard_map/reduce_scatter | solution.py:94
  203.7 3.3 copy-start.1
  203.7 3.5 copy-start.5
  210.0 1.0 copy-start.7
  272.3 46.6 %all-to-all-start.5 = ((bf16[64,2,128]{2,1,0:T(2,128)(2,1)}), bf16[64,2,128]{2,1,0:T(2,128)(2,1)S(1)}, u32[]{:S(2)}, u32[]{:S(2)}) async-start(bf16[64,2,128]{2,1,0:T(2,128)(2,1)} %bitcast.20), calls=%async_computation.6 | async-start | bytes 65536 | tf_op jit(solution)/shard_map/all_to_all | solution.py:47
  318.9 43.9 %all-to-all-start.4 = ((bf16[64,2,1792]{2,1,0:T(2,128)(2,1)}), bf16[64,2,1792]{2,1,0:T(2,128)(2,1)S(1)}, u32[]{:S(2)}, u32[]{:S(2)}) async-start(bf16[64,2,1792]{2,1,0:T(2,128)(2,1)} %reshape.53), calls=%async_computation.5 | async-start | bytes 917504 | tf_op jit(solution)/shard_map/all_to_all | solution.py:47
Sparse Core Ops, SparseCore 0:
  203.8 66.3 all-reduce.1
  273.0 43.8 reduce-scatter.1
